TPU v7x, 256 devices: a whole 4x4x8 slice. The times are simulated.
256 devices in a mesh: req: 32 (over z, x_hi, core), kvh: 4 (over y), exp: 2 (over x_lo).
Axes of the slice: x: 4 (x_hi: 2, x_lo: 2; x = x_hi * 2 + x_lo), y: 4, z: 8, core: 2. Of those that a mesh axis runs over, the one named last changes fastest.
Arguments:
- queries: bfloat16 [4096, 2048], P(('req', 'exp'), 'kvh'), may hold values from -170 to 170
- keys: bfloat16 [4096, 4, 64, 128], P(('req', 'exp'), 'kvh'), may hold values from -6 to 6
- values: bfloat16 [4096, 4, 64, 128], P(('req', 'exp'), 'kvh'), may hold values from -6 to 6
- lengths: int32 [4096], P('req'), may hold values from 2 to 64
- out_weight: bfloat16 [2048, 2048], P(('kvh', 'exp')), may hold values from -0.125 to 0.125
- residual: bfloat16 [4096, 2048], P('req'), may hold values from -54 to 54
- norm_gain: float32 [2048], replicated, may hold values from 0.5 to 2
- expert_ids: int32 [4096, 8], P('req'), may hold values from 0 to 63, as said below
- gate_weights: float32 [4096, 8], P('req'), may hold values from 0.2 to 1
- replica_map: int32 [128], replicated, may hold values from 0 to 63, as said below
- w_gate: bfloat16 [128, 2048, 384], P(('req', 'kvh'), None, 'exp')
- w_up: bfloat16 [128, 2048, 384], P(('req', 'kvh'), None, 'exp')
- w_down: bfloat16 [128, 384, 2048], P(('req', 'kvh'), 'exp')
Outputs:
- layer_out: bfloat16 [4096, 2048], P('req', ('kvh', 'exp'))
Inputs may be any that keep to these rules, and one draw needn't show every extreme that they name: `replica_map`: every one of the 64 experts is served by one or more slots; slots that serve one expert hold equal weights in w_gate, w_up and w_down. `expert_ids`: A token names 8 different experts and every expert is named by some token; among the 128 tokens of one req index no expert is named by more than 24 tokens, and in every req index some expert is named by exactly 24.
All inputs are finite; a program needn't handle non-finite values.
Results may differ from a plain program's by a relative error of at most 0.008.
Values may be sent and summed in bfloat16 or wider, within the bound.
A program may use at most 64 MiB of HBM per device.

v0:
```python
import jax
import jax.numpy as jnp
from jax import lax
from jax.sharding import PartitionSpec as P


def expert_runner(w_gate, w_up, w_down, complete, n_kvh, n_exp, block):

    def run(received):
        full = complete(received)
        lead_a = full.shape[0]
        lead_b = full.shape[1]
        d_model = w_gate.shape[1]
        rows = full.reshape(lead_a * lead_b, d_model)
        gate = jnp.dot(rows, w_gate[0], preferred_element_type=jnp.float32)
        up = jnp.dot(rows, w_up[0], preferred_element_type=jnp.float32)
        act = (jax.nn.silu(gate) * up).astype(jnp.bfloat16)
        down = jnp.dot(act, w_down[0], preferred_element_type=jnp.float32)
        terms = down.reshape(lead_a, lead_b, n_kvh, n_exp, block)
        summed = lax.psum_scatter(
            terms.astype(jnp.bfloat16), "exp", scatter_dimension=3, tiled=True
        )
        back = summed.reshape(lead_a, lead_b, n_kvh * block)
        return lax.all_to_all(back, "req", split_axis=0, concat_axis=0, tiled=True)

    return run


def shards(
    queries,
    keys,
    values,
    lengths,
    out_weight,
    residual,
    norm_gain,
    expert_ids,
    gate_weights,
    replica_map,
    w_gate,
    w_up,
    w_down,
):
    f32 = jnp.float32
    half_rows_count = queries.shape[0]
    n_rows = lengths.shape[0]
    head_dim = keys.shape[3]
    span = keys.shape[2]
    heads_here = queries.shape[1] // head_dim
    n_kvh = lax.axis_size("kvh")
    n_exp = lax.axis_size("exp")
    n_req = lax.axis_size("req")
    side = lax.axis_index("exp")
    own_lengths = lax.dynamic_slice_in_dim(lengths, side * half_rows_count, half_rows_count, 0)
    query = queries.reshape(half_rows_count, heads_here, head_dim)
    scores = jnp.einsum(
        "rhd,rpd->rhp", query, keys[:, 0], preferred_element_type=f32
    ) * head_dim ** (-0.5)
    position = lax.broadcasted_iota(jnp.int32, (1, 1, span), 2)
    valid = position < own_lengths[:, None, None]
    scores = jnp.where(valid, scores, -1e30)
    peak = jnp.max(scores, axis=-1)
    weights = jnp.where(valid, jnp.exp(scores - peak[..., None]), 0.0)
    total = jnp.sum(weights, axis=-1)
    probs = weights / total[..., None]
    numer = jnp.einsum(
        "rhp,rpd->rhd", probs, values[:, 0].astype(f32), precision=lax.Precision.HIGHEST
    )
    attended_part = numer.astype(jnp.bfloat16).reshape(half_rows_count, heads_here * head_dim)
    attended = lax.all_gather(attended_part, "exp", axis=0, tiled=True)
    cut = out_weight.shape[0]
    own_heads = lax.dynamic_slice_in_dim(attended, side * cut, cut, 1)
    d_model = out_weight.shape[1]
    block = d_model // (n_kvh * n_exp)
    attn_block = (
        lax.psum_scatter(
            lax.dot_general(
                out_weight, own_heads, (((0,), (1,)), ((), ())), preferred_element_type=f32
            ).astype(jnp.bfloat16),
            ("kvh", "exp"),
            scatter_dimension=0,
            tiled=True,
        )
        .astype(jnp.float32)
        .T
    )
    offset = lax.axis_index(("kvh", "exp")) * block
    mixed = lax.dynamic_slice_in_dim(residual, offset, block, 1).astype(f32) + attn_block
    squares = lax.psum(jnp.sum(mixed * mixed, axis=1), ("kvh", "exp"))
    scale = lax.rsqrt(squares / d_model + 1e-06)
    gain_block = lax.dynamic_slice_in_dim(norm_gain, offset, block, 0)
    normed = (mixed * scale[:, None] * gain_block[None, :]).astype(jnp.bfloat16)
    top = expert_ids.shape[1]
    n_slots = replica_map.shape[0]
    n_experts = n_slots // 2
    capacity = min(n_rows, max(2, (3 * n_rows * top + 2 * n_experts - 1) // (2 * n_experts)))
    probs_top = gate_weights / jnp.sum(gate_weights, axis=1, keepdims=True)
    expert_range = jnp.arange(n_experts, dtype=jnp.int32)
    owned = (replica_map[:, None] == expert_range[None, :]).astype(jnp.int32)
    earlier = jnp.cumsum(owned, axis=0) - owned
    rank = jnp.sum(earlier * owned, axis=1)
    copies = jnp.sum(owned, axis=0)
    picked = (expert_ids[..., None] == expert_range).astype(jnp.int32)
    copies_pair = jnp.sum(picked * copies, axis=-1)
    turn = jnp.full((n_rows, top), lax.axis_index("req"), jnp.int32)
    which = turn % copies_pair
    match = (replica_map == expert_ids[..., None]) & (rank == which[..., None])
    slot = jnp.argmax(match, axis=-1)
    mine = slot % n_kvh == lax.axis_index("kvh")
    flat_dest = (slot // n_kvh).reshape(-1)
    flat_mine = mine.reshape(-1)
    toward = (
        (flat_dest[:, None] == jnp.arange(n_req, dtype=jnp.int32)[None, :]) & flat_mine[:, None]
    ).astype(jnp.int32)
    before = jnp.cumsum(toward, axis=0) - toward
    place = jnp.sum(before * toward, axis=1)
    n_buffer = n_req * capacity
    target = jnp.where(flat_mine, flat_dest * capacity + place, n_buffer)
    row_of = jnp.arange(n_rows * top, dtype=jnp.int32) // top
    source = jnp.full((n_buffer,), -1, jnp.int32).at[target].set(row_of, mode="drop")
    full_rows = lax.all_gather(normed, ("kvh", "exp"), axis=1, tiled=True)

    def keep(received):
        return received

    runner = expert_runner(w_gate, w_up, w_down, keep, n_kvh, n_exp, block)
    taken = full_rows[jnp.maximum(source, 0)]
    returned = runner(
        lax.all_to_all(
            jnp.where(source[:, None] >= 0, taken, jnp.zeros((), jnp.bfloat16)).reshape(
                n_req, capacity, full_rows.shape[1]
            ),
            "req",
            split_axis=0,
            concat_axis=0,
            tiled=True,
        )
    )
    flat_back = returned.reshape(n_buffer, n_kvh * block)
    gathered = flat_back[jnp.minimum(target, n_buffer - 1)].reshape(n_rows, top, n_kvh * block)
    weight = jnp.where(mine, probs_top, 0.0)
    partial_value = jnp.zeros((n_rows, n_kvh * block), f32)
    for entry in range(top):
        partial_value = partial_value + weight[:, entry, None] * gathered[:, entry].astype(f32)
    moe_block = (
        lax.psum_scatter(
            partial_value.reshape(n_rows, n_kvh, block).astype(jnp.bfloat16),
            "kvh",
            scatter_dimension=1,
            tiled=True,
        )
        .astype(jnp.float32)
        .reshape(n_rows, block)
    )
    return (mixed + moe_block).astype(jnp.bfloat16)


def solution(mesh):
    in_specs = (
        P(("req", "exp"), "kvh"),
        P(("req", "exp"), "kvh", None, None),
        P(("req", "exp"), "kvh", None, None),
        P("req"),
        P(("kvh", "exp"), None),
        P("req", None),
        P(),
        P("req", None),
        P("req", None),
        P(),
        P(("req", "kvh"), None, "exp"),
        P(("req", "kvh"), None, "exp"),
        P(("req", "kvh"), "exp", None),
    )
    out_specs = P("req", ("kvh", "exp"))
    return jax.shard_map(shards, mesh=mesh, in_specs=in_specs, out_specs=out_specs, check_vma=False)
```

profile of v0, /device:TPU:2, one launch (start us, length us, event | category | flops | bytes accessed | tf_op | source)
XLA Modules:
  0.0 418.7 jit_solution(3520700671279704682)
XLA Ops:
  10.4 2.2 convolution_convert_fusion.2
  12.6 5.2 %all_gather.6 = bf16[128,512]{1,0:T(8,128)(2,1)S(1)} all-gather(bf16[64,512]{1,0:T(8,128)(2,1)S(1)} %bitcast.127), channel_id=1, replica_groups=mesh['req'=32,'kvh'=4,'exp'=2] {'exp'}, dimensions={0}, use_global_device_ids=true | all-gather | bytes 196608 | tf_op jit(solution)/shard_map/all_gather | solution.py:70
  19.9 5.6 %iota_reduce_fusion = (pred[128,8]{1,0:T(8,128)(4,1)}, s32[128,8]{1,0:T(8,128)S(1)}) fusion(s32[128,8]{1,0:T(8,128)S(1)} %copy.92, s32[128]{0:T(128)S(1)} %get-tuple-element.7, s32[128,8]{1,0:T(8,128)S(1)} %copy.91, s32[128]{0:T(128)S(1)} %copy-done.5), kind=kLoop, calls=%fused_computation.24 | loop fusion | flops 1303552 | bytes 14336 | tf_op jit(solution)/shard_map/shards/reduce | solution.py:108
  26.0 9.0 %reduce-window.6 = s32[32,8,128]{2,1,0:T(8,128)S(1)} reduce-window(s32[32,8,128]{2,1,0:T(8,128)S(1)} %fusion.21, s32[]{:T(128)} %constant.89.clone.1), window={size=1x1x128 pad=0_0x0_0x127_0}, to_apply=%region_9.10 | reduce-window | flops 4161536 | bytes 262148 | tf_op jit(solution)/shard_map/reduce-window
  36.1 4.3 %scatter_custom_fusion = s32[768]{0:T(1024)S(1)} fusion(s32[1024]{0:T(1024)S(1)} %bitcast.132, s32[1024]{0:T(1024)S(1)} %add_select_fusion, s32[]{:T(128)} %constant.107.clone.1), kind=kCustom, calls=%fused_computation.82 | custom fusion | bytes 3076 | tf_op jit(solution)/shard_map/scatter | solution.py:120
  41.3 18.5 %reduce-scatter.4.cloned.1.call-done = bf16[256,128]{0,1:T(8,128)(2,1)} async-done(((bf16[2048,128]{0,1:T(8,128)(2,1)}), bf16[256,128]{0,1:T(8,128)(2,1)}) %reduce-scatter.4.cloned.1.call-update) | async-done | bytes 65552 | tf_op jit(solution)/shard_map/reduce_scatter | solution.py:76
  60.8 19.4 %psum.7 = f32[128]{0:T(128)S(1)} all-reduce(f32[128]{0:T(128)S(1)} %multiply_reduce_fusion), channel_id=1, replica_groups=mesh['req'=32,'kvh'=4,'exp'=2] {'kvh','exp'}, use_global_device_ids=true, to_apply=%region_14.15 | all-reduce | flops 128 | bytes 1024 | tf_op jit(solution)/shard_map/psum | solution.py:89
  81.2 28.2 %all_gather.7 = bf16[128,2048]{1,0:T(8,128)(2,1)S(1)} all-gather(bf16[128,256]{1,0:T(8,128)(2,1)S(1)} %multiply_convert_fusion), channel_id=1, replica_groups=mesh['req'=32,'kvh'=4,'exp'=2] {'kvh','exp'}, dimensions={1}, use_global_device_ids=true | all-gather | bytes 589824 | tf_op jit(solution)/shard_map/all_gather | solution.py:121
  109.4 4.3 %gather_fusion = bf16[768,2048]{1,0:T(8,128)(2,1)} fusion(bf16[128,2048]{1,0:T(8,128)(2,1)S(1)} %all_gather.7, s32[1024]{0:T(1024)S(1)} %pad_clamp_fusion), kind=kCustom, calls=%fused_computation | custom fusion | bytes 6294528 | tf_op jit(solution)/shard_map/gather | solution.py:127
  113.7 3.8 broadcast_select_fusion
  117.5 8.9 %all-to-all-start = ((bf16[32,24,2048]{2,1,0:T(8,128)(2,1)}), bf16[32,24,2048]{2,1,0:T(8,128)(2,1)}, u32[]{:S(2)}, u32[]{:S(2)}) async-start(bf16[32,24,2048]{2,1,0:T(8,128)(2,1)} %broadcast_select_fusion), calls=%async_computation.1 | async-start | bytes 6291456 | tf_op jit(solution)/shard_map/all_to_all | solution.py:129
  127.2 73.4 %all-to-all-done = bf16[32,24,2048]{2,1,0:T(8,128)(2,1)} async-done(((bf16[32,24,2048]{2,1,0:T(8,128)(2,1)}), bf16[32,24,2048]{2,1,0:T(8,128)(2,1)}, u32[]{:S(2)}, u32[]{:S(2)}) %all-to-all-start) | async-done | bytes 3145760 | tf_op jit(solution)/shard_map/all_to_all | solution.py:129
  200.6 3.2 fusion.11
  203.8 3.1 fusion.2
  207.1 2.7 convolution_convert_fusion.1
  210.4 92.4 %all-reduce.3.cloned.1.call-done = bf16[32,24,4,2,256]{4,1,3,2,0:T(8,128)(2,1)} async-done(((bf16[32,24,4,2,256]{4,1,3,2,0:T(8,128)(2,1)}), bf16[32,24,4,2,256]{4,1,3,2,0:T(8,128)(2,1)}) %all-reduce.3.cloned.1.call-update) | async-done | bytes 3145744
  302.8 2.2 constant_dynamic-slice_fusion
  305.8 2.4 reshape.238
  308.1 9.5 %all-to-all-start.1 = ((bf16[32,24,1024]{2,1,0:T(8,128)(2,1)}), bf16[32,24,1024]{2,1,0:T(8,128)(2,1)S(1)}, u32[]{:S(2)}, u32[]{:S(2)}) async-start(bf16[32,24,1024]{2,1,0:T(8,128)(2,1)} %reshape.238), calls=%async_computation.2 | async-start | bytes 3145728 | tf_op jit(solution)/shard_map/all_to_all | solution.py:24
  317.7 39.4 %all-to-all-done.1 = bf16[32,24,1024]{2,1,0:T(8,128)(2,1)S(1)} async-done(((bf16[32,24,1024]{2,1,0:T(8,128)(2,1)}), bf16[32,24,1024]{2,1,0:T(8,128)(2,1)S(1)}, u32[]{:S(2)}, u32[]{:S(2)}) %all-to-all-start.1) | async-done | bytes 1572896 | tf_op jit(solution)/shard_map/all_to_all | solution.py:24
  357.0 5.4 %gather_fusion.1 = bf16[1024,1024]{1,0:T(8,128)(2,1)} fusion(bf16[768,1024]{1,0:T(8,128)(2,1)S(1)} %bitcast.113, s32[1024]{0:T(1024)S(1)} %broadcast_clamp_fusion), kind=kCustom, calls=%fused_computation.1 | custom fusion | bytes 4198400 | tf_op jit(solution)/shard_map/gather | solution.py:140
  362.4 12.5 %fusion.38 = (bf16[128,1,1024]{2,1,0:T(2,128)(2,1)S(1)}, bf16[128,1,1024]{2,1,0:T(2,128)(2,1)}, bf16[128,1,1024]{2,1,0:T(2,128)(2,1)}, bf16[128,1,1024]{2,1,0:T(...) fusion(bf16[128,8,1024]{2,1,0:T(8,128)(2,1)} %bitcast.114), kind=kLoop, calls=%fused_computation.95 | loop fusion | bytes 4194304 | tf_op jit(solution)/shard_map/slice | solution.py:144
  386.3 2.6 add_convert_fusion
  388.9 21.7 %reduce-scatter.6.cloned.1.call-done = bf16[128,1,256]{2,0,1:T(8,128)(2,1)} async-done(((bf16[128,4,256]{2,0,1:T(8,128)(2,1)}), bf16[128,1,256]{2,0,1:T(8,128)(2,1)}) %reduce-scatter.6.cloned.1.call-update) | async-done | bytes 65552 | tf_op jit(solution)/shard_map/reduce_scatter | solution.py:146
  (91 shorter events, 25.5 us)
Async XLA Ops:
  6.5 11.3 %copy-start = (bf16[256,2048]{1,0:T(8,128)(2,1)S(1)}, bf16[256,2048]{1,0:T(8,128)(2,1)}, u32[]{:S(2)}) copy-start(bf16[256,2048]{1,0:T(8,128)(2,1)} %param.17) | copy-start | bytes 3145732
  6.5 12.4 %copy-start.5 = (s32[128]{0:T(128)S(1)}, s32[128]{0:T(128)}, u32[]{:S(2)}) copy-start(s32[128]{0:T(128)} %param.22) | copy-start | bytes 1540
  6.5 12.9 %copy-start.4 = (s32[128,8]{0,1:T(8,128)S(1)}, s32[128,8]{0,1:T(8,128)}, u32[]{:S(2)}) copy-start(s32[128,8]{0,1:T(8,128)} %param.20) | copy-start | bytes 12292
  6.5 19.0 %copy-start.3 = (f32[128,8]{0,1:T(8,128)S(1)}, f32[128,8]{0,1:T(8,128)}, u32[]{:S(2)}) copy-start(f32[128,8]{0,1:T(8,128)} %param.21) | copy-start | bytes 12292
  6.5 53.3 %reduce-scatter.4.cloned.1.call-start = ((), (), s32[]{:S(2)}) async-start(), calls=%async_computation.4 | async-start | bytes 589824 | tf_op jit(solution)/shard_map/reduce_scatter | solution.py:76
  117.5 9.1 %copy-start.1 = (bf16[1,192,2048]{2,1,0:T(8,128)(2,1)S(1)}, bf16[1,192,2048]{2,1,0:T(8,128)(2,1)}, u32[]{:S(2)}) copy-start(bf16[1,192,2048]{2,1,0:T(8,128)(2,1)} %param.25) | copy-start | bytes 2359300
  117.5 83.1 %copy-start.6 = (bf16[1,2048,192]{1,2,0:T(8,128)(2,1)S(1)}, bf16[1,2048,192]{1,2,0:T(8,128)(2,1)}, u32[]{:S(2)}) copy-start(bf16[1,2048,192]{1,2,0:T(8,128)(2,1)} %param.23) | copy-start | bytes 2359300
  117.5 83.1 %all-to-all-start = ((bf16[32,24,2048]{2,1,0:T(8,128)(2,1)}), bf16[32,24,2048]{2,1,0:T(8,128)(2,1)}, u32[]{:S(2)}, u32[]{:S(2)}) async-start(bf16[32,24,2048]{2,1,0:T(8,128)(2,1)} %broadcast_select_fusion), calls=%async_computation.1 | async-start | bytes 6291456 | tf_op jit(solution)/shard_map/all_to_all | solution.py:129
  126.4 176.5 %all-reduce.3.cloned.1.call-start = ((), (), s32[]{:S(2)}) async-start(), calls=%async_computation.6 | async-start | bytes 6291456
  200.6 3.2 copy-start.7
  207.1 2.8 copy-start.8
  308.1 48.9 %all-to-all-start.1 = ((bf16[32,24,1024]{2,1,0:T(8,128)(2,1)}), bf16[32,24,1024]{2,1,0:T(8,128)(2,1)S(1)}, u32[]{:S(2)}, u32[]{:S(2)}) async-start(bf16[32,24,1024]{2,1,0:T(8,128)(2,1)} %reshape.238), calls=%async_computation.2 | async-start | bytes 3145728 | tf_op jit(solution)/shard_map/all_to_all | solution.py:24
  317.6 93.0 %reduce-scatter.6.cloned.1.call-start = ((), (), s32[]{:S(2)}) async-start(), calls=%async_computation.5 | async-start | bytes 327680 | tf_op jit(solution)/shard_map/reduce_scatter | solution.py:146
  385.7 24.9 %copy-start.2 = (bf16[256,128]{0,1:T(8,128)(2,1)S(1)}, bf16[256,128]{0,1:T(8,128)(2,1)}, u32[]{:S(2)}) copy-start(bf16[256,128]{0,1:T(8,128)(2,1)} %reduce-scatter.4.cloned.1.call-done) | copy-start | bytes 196612
Sparse Core Ops, SparseCore 0:
  19.1 40.6 reduce-scatter.3
  209.9 92.8 all-reduce.2
  389.0 21.5 reduce-scatter.5
where the time goes:
time: 419 us
  waiting for transfers between devices  246 us (59%)
  blocking collectives  52.8 us (13%)
  local copies, waits for them, and re-layouts  48.4 us (12%)
  other arithmetic  25.5 us (6%)
  starting transfers between devices  18.6 us (4%)
  matrix products  14.4 us (3%)
  between operations  13.5 us (3%)
    unnamed x4, waiting for transfers between devices  92.5 us
    all_to_all x1, waiting for transfers between devices, shards(): lax.all_to_all(jnp.where(source[:, None] >= 0, taken, jnp.zeros((), jnp.b...  73.4 us
    all_to_all x1, waiting for transfers between devices, run(): return lax.all_to_all(back, 'req', split_axis=0, concat_axis=0, tiled=True)  39.4 us
    all_gather x1, blocking collectives, shards(): full_rows = lax.all_gather(normed, ('kvh', 'exp'), axis=1, tiled=True)  28.2 us
    reduce_scatter x1, waiting for transfers between devices, shards(): lax.psum_scatter(partial_value.reshape(n_rows, n_kvh, block).astype(jnp.b...  21.7 us
    psum x1, blocking collectives, shards(): squares = lax.psum(jnp.sum(mixed * mixed, axis=1), ('kvh', 'exp'))  19.4 us
    reduce_scatter x1, waiting for transfers between devices, shards(): lax.psum_scatter(lax.dot_general(out_weight, own_heads, (((0,), (1,)), ((...  18.5 us
    slice x1, local copies, waits for them, and re-layouts, shards(): gathered[:, entry].astype(f32)  12.5 us
  transfers between devices with their start and end apart: 5, of which 5 were waited for; matrix products, arithmetic and copies ran while one was open for 6% of the time, Pallas kernels for 0%

commit v1 on v0

--- a/solution.py
+++ b/solution.py
@@ -118,7 +118,10 @@
     target = jnp.where(flat_mine, flat_dest * capacity + place, n_buffer)
     row_of = jnp.arange(n_rows * top, dtype=jnp.int32) // top
     source = jnp.full((n_buffer,), -1, jnp.int32).at[target].set(row_of, mode="drop")
-    full_rows = lax.all_gather(normed, ("kvh", "exp"), axis=1, tiled=True)
+    full_rows = jnp.concatenate(
+        lax.all_to_all(jnp.stack([normed] * lax.axis_size(("kvh", "exp"))), ("kvh", "exp"), 0, 0),
+        axis=1,
+    )
 
     def keep(received):
         return received

time: 419 us -> 403 us (0.962)
  blocking collectives: 52.8 us -> 24.8 us
  waiting for transfers between devices: 246 us -> 252 us
  starting transfers between devices: 18.6 us -> 23.1 us
    all_gather x1 -> x0, blocking collectives: 28.2 us -> none  [shards(): full_rows = lax.all_gather(normed, ('kvh', 'exp'), axis=1, tiled=True)]
    all_to_all x0 -> x1, waiting for transfers between devices: none -> 7.42 us  [shards(): lax.all_to_all(jnp.stack([normed] * lax.axis_size(('kvh', 'exp'))), ('kvh...]
  transfers between devices with their start and end apart: 5 -> 6, of which waited for: 5 -> 6; matrix products, arithmetic and copies ran while one was open for 6% -> 6% of each run, Pallas kernels for 0% -> 0%
where the time goes in v1:
time: 403 us; the launch traced here: 402 us
  waiting for transfers between devices  252 us (63%)
  local copies, waits for them, and re-layouts  49.3 us (12%)
  other arithmetic  25.5 us (6%)
  blocking collectives  24.8 us (6%)
  starting transfers between devices  23.1 us (6%)
  matrix products  14.4 us (4%)
  between operations  13.5 us (3%)
    unnamed x4, waiting for transfers between devices  91.1 us
    all_to_all x1, waiting for transfers between devices, shards(): lax.all_to_all(jnp.where(source[:, None] >= 0, taken, jnp.zeros((), jnp.b...  73.4 us
    all_to_all x1, waiting for transfers between devices, run(): return lax.all_to_all(back, 'req', split_axis=0, concat_axis=0, tiled=True)  39.4 us
    reduce_scatter x1, waiting for transfers between devices, shards(): lax.psum_scatter(partial_value.reshape(n_rows, n_kvh, block).astype(jnp.b...  21.7 us
    psum x1, blocking collectives, shards(): squares = lax.psum(jnp.sum(mixed * mixed, axis=1), ('kvh', 'exp'))  19.6 us
    reduce_scatter x1, waiting for transfers between devices, shards(): lax.psum_scatter(lax.dot_general(out_weight, own_heads, (((0,), (1,)), ((...  18.6 us
    slice x1, local copies, waits for them, and re-layouts, shards(): gathered[:, entry].astype(f32)  12.5 us
    unnamed x30, local copies, waits for them, and re-layouts  9.82 us
  transfers between devices with their start and end apart: 6, of which 6 were waited for; matrix products, arithmetic and copies ran while one was open for 6% of the time, Pallas kernels for 0%

profile of v1, /device:TPU:2, one launch (start us, length us, event | category | flops | bytes accessed | tf_op | source)
XLA Modules:
  0.0 402.3 jit_solution(410025781096947493)
XLA Ops:
  10.4 2.2 convolution_convert_fusion.2
  12.6 5.2 %all_gather.3 = bf16[128,512]{1,0:T(8,128)(2,1)S(1)} all-gather(bf16[64,512]{1,0:T(8,128)(2,1)S(1)} %bitcast.132), channel_id=1, replica_groups=mesh['req'=32,'kvh'=4,'exp'=2] {'exp'}, dimensions={0}, use_global_device_ids=true | all-gather | bytes 196608 | tf_op jit(solution)/shard_map/all_gather | solution.py:70
  19.9 5.6 %iota_reduce_fusion = (pred[128,8]{1,0:T(8,128)(4,1)}, s32[128,8]{1,0:T(8,128)S(1)}) fusion(s32[128,8]{1,0:T(8,128)S(1)} %copy.93, s32[128]{0:T(128)S(1)} %get-tuple-element.7, s32[128,8]{1,0:T(8,128)S(1)} %copy.92, s32[128]{0:T(128)S(1)} %copy-done.5), kind=kLoop, calls=%fused_computation.24 | loop fusion | flops 1303552 | bytes 14336 | tf_op jit(solution)/shard_map/shards/reduce | solution.py:108
  26.3 9.0 %reduce-window.6 = s32[32,8,128]{2,1,0:T(8,128)S(1)} reduce-window(s32[32,8,128]{2,1,0:T(8,128)S(1)} %fusion.21, s32[]{:T(128)} %constant.89.clone.1), window={size=1x1x128 pad=0_0x0_0x127_0}, to_apply=%region_9.10 | reduce-window | flops 4161536 | bytes 262148 | tf_op jit(solution)/shard_map/reduce-window
  36.8 4.3 %scatter_custom_fusion = s32[768]{0:T(1024)S(1)} fusion(s32[1024]{0:T(1024)S(1)} %bitcast.137, s32[1024]{0:T(1024)S(1)} %add_select_fusion, s32[]{:T(128)} %constant.107.clone.1), kind=kCustom, calls=%fused_computation.82 | custom fusion | bytes 3076 | tf_op jit(solution)/shard_map/scatter | solution.py:120
  41.1 18.6 %reduce-scatter.4.cloned.1.call-done = bf16[256,128]{0,1:T(8,128)(2,1)} async-done(((bf16[2048,128]{0,1:T(8,128)(2,1)}), bf16[256,128]{0,1:T(8,128)(2,1)}) %reduce-scatter.4.cloned.1.call-update) | async-done | bytes 65552 | tf_op jit(solution)/shard_map/reduce_scatter | solution.py:76
  60.7 19.6 %psum.7 = f32[128]{0:T(128)S(1)} all-reduce(f32[128]{0:T(128)S(1)} %multiply_reduce_fusion), channel_id=1, replica_groups=mesh['req'=32,'kvh'=4,'exp'=2] {'kvh','exp'}, use_global_device_ids=true, to_apply=%region_14.15 | all-reduce | flops 128 | bytes 1024 | tf_op jit(solution)/shard_map/psum | solution.py:89
  82.1 4.0 %all-to-all-start = ((bf16[8,128,256]{2,1,0:T(8,128)(2,1)}), bf16[8,128,256]{2,1,0:T(8,128)(2,1)S(1)}, u32[]{:S(2)}, u32[]{:S(2)}) async-start(bf16[8,128,256]{2,1,0:T(8,128)(2,1)} %stack.2), calls=%async_computation.1 | async-start | bytes 1048576 | tf_op jit(solution)/shard_map/all_to_all | solution.py:122
  86.3 7.4 %all-to-all-done = bf16[8,128,256]{2,1,0:T(8,128)(2,1)S(1)} async-done(((bf16[8,128,256]{2,1,0:T(8,128)(2,1)}), bf16[8,128,256]{2,1,0:T(8,128)(2,1)S(1)}, u32[]{:S(2)}, u32[]{:S(2)}) %all-to-all-start) | async-done | bytes 524320 | tf_op jit(solution)/shard_map/all_to_all | solution.py:122
  93.8 4.3 %gather_fusion = bf16[768,2048]{1,0:T(8,128)(2,1)} fusion(bf16[128,2048]{1,0:T(8,128)(2,1)S(1)} %bitcast.116, s32[1024]{0:T(1024)S(1)} %pad_clamp_fusion), kind=kCustom, calls=%fused_computation | custom fusion | bytes 6294528 | tf_op jit(solution)/shard_map/gather | solution.py:130
  98.0 3.8 broadcast_select_fusion
  101.9 9.3 %all-to-all-start.1 = ((bf16[32,24,2048]{2,1,0:T(8,128)(2,1)}), bf16[32,24,2048]{2,1,0:T(8,128)(2,1)}, u32[]{:S(2)}, u32[]{:S(2)}) async-start(bf16[32,24,2048]{2,1,0:T(8,128)(2,1)} %broadcast_select_fusion), calls=%async_computation.2 | async-start | bytes 6291456 | tf_op jit(solution)/shard_map/all_to_all | solution.py:132
  112.1 73.4 %all-to-all-done.1 = bf16[32,24,2048]{2,1,0:T(8,128)(2,1)} async-done(((bf16[32,24,2048]{2,1,0:T(8,128)(2,1)}), bf16[32,24,2048]{2,1,0:T(8,128)(2,1)}, u32[]{:S(2)}, u32[]{:S(2)}) %all-to-all-start.1) | async-done | bytes 3145760 | tf_op jit(solution)/shard_map/all_to_all | solution.py:132
  185.5 3.1 fusion.11
  188.7 3.1 fusion.2
  192.0 2.7 convolution_convert_fusion.1
  195.3 91.1 %all-reduce.3.cloned.1.call-done = bf16[32,24,4,2,256]{4,1,3,2,0:T(8,128)(2,1)} async-done(((bf16[32,24,4,2,256]{4,1,3,2,0:T(8,128)(2,1)}), bf16[32,24,4,2,256]{4,1,3,2,0:T(8,128)(2,1)}) %all-reduce.3.cloned.1.call-update) | async-done | bytes 3145744
  289.4 2.4 reshape.248
  291.7 9.5 %all-to-all-start.2 = ((bf16[32,24,1024]{2,1,0:T(8,128)(2,1)}), bf16[32,24,1024]{2,1,0:T(8,128)(2,1)S(1)}, u32[]{:S(2)}, u32[]{:S(2)}) async-start(bf16[32,24,1024]{2,1,0:T(8,128)(2,1)} %reshape.248), calls=%async_computation.3 | async-start | bytes 3145728 | tf_op jit(solution)/shard_map/all_to_all | solution.py:24
  301.2 39.4 %all-to-all-done.2 = bf16[32,24,1024]{2,1,0:T(8,128)(2,1)S(1)} async-done(((bf16[32,24,1024]{2,1,0:T(8,128)(2,1)}), bf16[32,24,1024]{2,1,0:T(8,128)(2,1)S(1)}, u32[]{:S(2)}, u32[]{:S(2)}) %all-to-all-start.2) | async-done | bytes 1572896 | tf_op jit(solution)/shard_map/all_to_all | solution.py:24
  340.6 5.4 %gather_fusion.1 = bf16[1024,1024]{1,0:T(8,128)(2,1)} fusion(bf16[768,1024]{1,0:T(8,128)(2,1)S(1)} %bitcast.117, s32[1024]{0:T(1024)S(1)} %broadcast_clamp_fusion), kind=kCustom, calls=%fused_computation.1 | custom fusion | bytes 4198400 | tf_op jit(solution)/shard_map/gather | solution.py:143
  346.0 12.5 %fusion.38 = (bf16[128,1,1024]{2,1,0:T(2,128)(2,1)S(1)}, bf16[128,1,1024]{2,1,0:T(2,128)(2,1)}, bf16[128,1,1024]{2,1,0:T(2,128)(2,1)}, bf16[128,1,1024]{2,1,0:T(...) fusion(bf16[128,8,1024]{2,1,0:T(8,128)(2,1)} %bitcast.118), kind=kLoop, calls=%fused_computation.95 | loop fusion | bytes 4194304 | tf_op jit(solution)/shard_map/slice | solution.py:147
  369.8 2.6 add_convert_fusion
  372.5 21.7 %reduce-scatter.6.cloned.1.call-done = bf16[128,1,256]{2,0,1:T(8,128)(2,1)} async-done(((bf16[128,4,256]{2,0,1:T(8,128)(2,1)}), bf16[128,1,256]{2,0,1:T(8,128)(2,1)}) %reduce-scatter.6.cloned.1.call-update) | async-done | bytes 65552 | tf_op jit(solution)/shard_map/reduce_scatter | solution.py:149
  (94 shorter events, 28.5 us)
Async XLA Ops:
  6.5 11.3 %copy-start = (bf16[256,2048]{1,0:T(8,128)(2,1)S(1)}, bf16[256,2048]{1,0:T(8,128)(2,1)}, u32[]{:S(2)}) copy-start(bf16[256,2048]{1,0:T(8,128)(2,1)} %param.17) | copy-start | bytes 3145732
  6.5 12.4 %copy-start.5 = (s32[128]{0:T(128)S(1)}, s32[128]{0:T(128)}, u32[]{:S(2)}) copy-start(s32[128]{0:T(128)} %param.22) | copy-start | bytes 1540
  6.5 12.9 %copy-start.4 = (s32[128,8]{0,1:T(8,128)S(1)}, s32[128,8]{0,1:T(8,128)}, u32[]{:S(2)}) copy-start(s32[128,8]{0,1:T(8,128)} %param.20) | copy-start | bytes 12292
  6.5 18.9 %copy-start.3 = (f32[128,8]{0,1:T(8,128)S(1)}, f32[128,8]{0,1:T(8,128)}, u32[]{:S(2)}) copy-start(f32[128,8]{0,1:T(8,128)} %param.21) | copy-start | bytes 12292
  6.5 53.2 %reduce-scatter.4.cloned.1.call-start = ((), (), s32[]{:S(2)}) async-start(), calls=%async_computation.5 | async-start | bytes 589824 | tf_op jit(solution)/shard_map/reduce_scatter | solution.py:76
  82.1 11.6 %all-to-all-start = ((bf16[8,128,256]{2,1,0:T(8,128)(2,1)}), bf16[8,128,256]{2,1,0:T(8,128)(2,1)S(1)}, u32[]{:S(2)}, u32[]{:S(2)}) async-start(bf16[8,128,256]{2,1,0:T(8,128)(2,1)} %stack.2), calls=%async_computation.1 | async-start | bytes 1048576 | tf_op jit(solution)/shard_map/all_to_all | solution.py:122
  101.9 9.6 %copy-start.1 = (bf16[1,192,2048]{2,1,0:T(8,128)(2,1)S(1)}, bf16[1,192,2048]{2,1,0:T(8,128)(2,1)}, u32[]{:S(2)}) copy-start(bf16[1,192,2048]{2,1,0:T(8,128)(2,1)} %param.25) | copy-start | bytes 2359300
  101.9 83.6 %copy-start.6 = (bf16[1,2048,192]{1,2,0:T(8,128)(2,1)S(1)}, bf16[1,2048,192]{1,2,0:T(8,128)(2,1)}, u32[]{:S(2)}) copy-start(bf16[1,2048,192]{1,2,0:T(8,128)(2,1)} %param.23) | copy-start | bytes 2359300
  101.9 83.6 %all-to-all-start.1 = ((bf16[32,24,2048]{2,1,0:T(8,128)(2,1)}), bf16[32,24,2048]{2,1,0:T(8,128)(2,1)}, u32[]{:S(2)}, u32[]{:S(2)}) async-start(bf16[32,24,2048]{2,1,0:T(8,128)(2,1)} %broadcast_select_fusion), calls=%async_computation.2 | async-start | bytes 6291456 | tf_op jit(solution)/shard_map/all_to_all | solution.py:132
  111.2 175.2 %all-reduce.3.cloned.1.call-start = ((), (), s32[]{:S(2)}) async-start(), calls=%async_computation.7 | async-start | bytes 6291456
  185.5 3.2 copy-start.7
  191.9 2.8 copy-start.8
  291.7 48.9 %all-to-all-start.2 = ((bf16[32,24,1024]{2,1,0:T(8,128)(2,1)}), bf16[32,24,1024]{2,1,0:T(8,128)(2,1)S(1)}, u32[]{:S(2)}, u32[]{:S(2)}) async-start(bf16[32,24,1024]{2,1,0:T(8,128)(2,1)} %reshape.248), calls=%async_computation.3 | async-start | bytes 3145728 | tf_op jit(solution)/shard_map/all_to_all | solution.py:24
  301.2 93.0 %reduce-scatter.6.cloned.1.call-start = ((), (), s32[]{:S(2)}) async-start(), calls=%async_computation.6 | async-start | bytes 327680 | tf_op jit(solution)/shard_map/reduce_scatter | solution.py:149
  369.2 24.9 %copy-start.2 = (bf16[256,128]{0,1:T(8,128)(2,1)S(1)}, bf16[256,128]{0,1:T(8,128)(2,1)}, u32[]{:S(2)}) copy-start(bf16[256,128]{0,1:T(8,128)(2,1)} %reduce-scatter.4.cloned.1.call-done) | copy-start | bytes 196612
Sparse Core Ops, SparseCore 0:
  19.1 40.6 reduce-scatter.3
  194.8 91.5 all-reduce.2
  372.6 21.5 reduce-scatter.5
